TPU v7x, 32 devices: a whole 2x2x4 slice. The times are simulated.
32 devices in a mesh: enc: 4 (over z), ctx: 8 (over y, x, core).
Axes of the slice: x: 2, y: 2, z: 4, core: 2. Of those that a mesh axis runs over, the one named last changes fastest.
Arguments:
- patches: bfloat16 [3072, 1280], P('enc'), may hold values from -17 to 17
- patch_image: int32 [3072], P('enc'), may hold values from 63 to 767, as said below
- vit_gain: float32 [1280], replicated, may hold values from 0.1 to 1.9
- vit_qkv: bfloat16 [1280, 16, 240], P(None, 'ctx')
- vit_proj: bfloat16 [1280, 1280], P('ctx'), may hold values from -0.15625 to 0.15625
- merge_gain: float32 [1280], replicated, may hold values from 0.1 to 1.9
- merge_up: bfloat16 [5120, 5120], P(None, 'ctx'), may hold values from -0.078125 to 0.078125
- merge_down: bfloat16 [5120, 8192], P('ctx', 'enc'), may hold values from -0.078125 to 0.078125
- text_embed: bfloat16 [3072, 8192], P('ctx', 'enc'), may hold values from -17 to 17
- placeholder_unit: int32 [3072], replicated, may hold values from -1 to 767, as said below
- doc_id: int32 [3072], replicated, may hold values from 0 to 15, never falling along the last dimension, each value on 1 to 1920 neighbouring positions
- dec_gain: float32 [8192], replicated, may hold values from 0.1 to 1.9
- dec_wq: bfloat16 [8192, 2048], P(None, 'enc')
- dec_wk: bfloat16 [8192, 512], P(None, 'enc')
- dec_wv: bfloat16 [8192, 512], P(None, 'enc'), may hold values from -0.0625 to 0.0625
Outputs:
- attended: bfloat16 [3072, 2048], P('ctx', 'enc')
Inputs may be any that keep to these rules, and one draw needn't show every extreme that they name: `patch_image`: the patches of an image are consecutive, start at a multiple of 4, number a multiple of 4 and at most 256, and lie within one aligned block of 768 patches; image numbers never fall and differ between images; in every such block some image has exactly 256 patches. `placeholder_unit`: -1 marks a text position. Every unit appears exactly once; the units of one image fill consecutive placeholders in their order; the placeholders of an aligned block of 384 positions are consecutive and number at most 192, and some block holds exactly 192. `doc_id`: document numbers never fall; a document has at most 1920 positions, and some document exactly 1920.
All inputs are finite; a program needn't handle non-finite values.
Results may differ from a plain program's by a relative error of at most 0.0085.
Values may be sent and summed in bfloat16 or wider, within the bound.
No kernel may reach another device: no remote copies, remote signals or barrier semaphores. Data moves between devices by JAX's collectives and lax.ppermute only.
A program may use at most 128 MiB of HBM per device.

v0:
```python
import math
import jax
import jax.numpy as jnp
from jax import lax
from jax.sharding import PartitionSpec as P

HD = 128
QPK = 4
EPSILON = 1e-06
NEGATIVE = -1e30


def layer_norm(values, scaling):
    widened = values.astype(jnp.float32)
    center = widened - jnp.mean(widened, axis=1, keepdims=True)
    spread = jnp.mean(center * center, axis=1, keepdims=True)
    return (center * lax.rsqrt(spread + EPSILON) * scaling).astype(jnp.bfloat16)


def image_attention(queries, keys_in, values_in, image_ids):
    head_count, row_count, head_width = queries.shape
    block_rows = math.gcd(row_count, 512)
    scaling = head_width ** (-0.5)

    def image_one_block(offset):
        query_block = lax.dynamic_slice_in_dim(queries, offset, block_rows, 1)
        block_ids = lax.dynamic_slice_in_dim(image_ids, offset, block_rows, 0)
        allowed = block_ids[:, None] == image_ids[None, :]
        scores = (
            jnp.einsum("hqd,hkd->hqk", query_block, keys_in, preferred_element_type=jnp.float32)
            * scaling
        )
        scores = jnp.where(allowed[None], scores, NEGATIVE)
        highest = jnp.max(scores, axis=2, keepdims=True)
        weights = jnp.exp(scores - highest)
        totals = jnp.sum(weights, axis=2, keepdims=True)
        mixture = jnp.einsum(
            "hqk,hkd->hqd",
            weights.astype(jnp.bfloat16),
            values_in,
            preferred_element_type=jnp.float32,
        )
        return (mixture / totals).astype(jnp.bfloat16)

    offsets = jnp.arange(row_count // block_rows, dtype=jnp.int32) * block_rows
    blocks = lax.map(image_one_block, offsets)
    return blocks.transpose(1, 0, 2, 3).reshape(head_count, row_count, head_width)


def body(
    patches,
    patch_image,
    vit_gain,
    vit_qkv,
    vit_proj,
    merge_gain,
    merge_up,
    merge_down,
    text_embed,
    placeholder_unit,
    doc_id,
    dec_gain,
    dec_wq,
    dec_wk,
    dec_wv,
):
    ctx_index = lax.axis_index("ctx")
    group_rows = patches.shape[0]
    head_count = vit_qkv.shape[1]
    head_width = vit_qkv.shape[2] // 3
    normed_patches = layer_norm(patches, vit_gain)
    packed = jnp.dot(
        normed_patches,
        vit_qkv.reshape(vit_qkv.shape[0], head_count * 3 * head_width),
        preferred_element_type=jnp.float32,
    )
    packed = (
        packed.astype(jnp.bfloat16)
        .reshape(group_rows, head_count, 3, head_width)
        .transpose(2, 1, 0, 3)
    )
    attended_patches = image_attention(packed[0], packed[1], packed[2], patch_image)
    flat_heads = attended_patches.transpose(1, 0, 2).reshape(group_rows, head_count * head_width)
    head_terms = jnp.dot(flat_heads, vit_proj, preferred_element_type=jnp.float32)
    summed = lax.psum(head_terms, "ctx")
    vit_out = (patches.astype(jnp.float32) + summed).astype(jnp.bfloat16)
    merge_input = layer_norm(lax.optimization_barrier(vit_out), merge_gain)
    unit_inputs = merge_input.reshape(group_rows // 4, 4 * merge_input.shape[1])
    hidden = jax.nn.gelu(
        jnp.dot(unit_inputs, merge_up, preferred_element_type=jnp.float32), approximate=False
    ).astype(jnp.bfloat16)
    all_hidden = lax.all_gather(hidden, "enc", axis=0, tiled=True)
    unit_total = all_hidden.shape[0]
    tok_rows = text_embed.shape[0]
    local_units = lax.dynamic_slice_in_dim(placeholder_unit, ctx_index * tok_rows, tok_rows, 0)
    present = local_units >= 0
    own_vision = lax.psum_scatter(
        jnp.dot(all_hidden, merge_down, preferred_element_type=jnp.float32),
        "ctx",
        scatter_dimension=0,
        tiled=True,
    ).astype(jnp.bfloat16)
    vision_all = lax.all_gather(own_vision, "ctx", axis=0, tiled=True)
    vision_local = jnp.take(vision_all, jnp.clip(local_units, 0, unit_total - 1), axis=0)
    sequence = jnp.where(present[:, None], vision_local, text_embed)
    full_rows = lax.all_gather(sequence, "enc", axis=1, tiled=True)
    widened = full_rows.astype(jnp.float32)
    row_scale = lax.rsqrt(jnp.mean(widened * widened, axis=1, keepdims=True) + EPSILON)
    normed = (widened * row_scale * dec_gain).astype(jnp.bfloat16)
    queries_flat = jnp.dot(normed, dec_wq, preferred_element_type=jnp.float32).astype(jnp.bfloat16)
    keys_local = jnp.dot(normed, dec_wk, preferred_element_type=jnp.float32).astype(jnp.bfloat16)
    values_local = jnp.dot(normed, dec_wv, preferred_element_type=jnp.float32).astype(jnp.bfloat16)
    kv_local = dec_wk.shape[1] // HD
    queries = queries_flat.reshape(tok_rows, kv_local, QPK, HD).transpose(1, 2, 0, 3)
    query_first = ctx_index * tok_rows
    query_pos = query_first + jnp.arange(tok_rows, dtype=jnp.int32)
    query_docs = lax.dynamic_slice_in_dim(doc_id, query_first, tok_rows, 0)
    scaling = HD ** (-0.5)
    start_state = (
        jnp.full((kv_local, QPK, tok_rows), NEGATIVE, jnp.float32),
        jnp.zeros((kv_local, QPK, tok_rows), jnp.float32),
        jnp.zeros((kv_local, QPK, tok_rows, HD), jnp.float32),
    )
    offset = jnp.int32(0)
    key_part = lax.all_gather(keys_local, "ctx", axis=0, tiled=True)
    value_part = lax.all_gather(values_local, "ctx", axis=0, tiled=True)
    key_count = key_part.shape[0]
    sub_rows = math.gcd(key_count, 512)
    last_doc = lax.dynamic_slice_in_dim(doc_id, offset + key_count - 1, 1, 0)[0]
    visible = (offset <= query_first + tok_rows - 1) & (last_doc >= query_docs[0])

    def update(current):

        def update_one_block(turn_index, inner_state):
            highest, totals, mixture = inner_state
            begin_row = turn_index * sub_rows
            keys_block = lax.dynamic_slice_in_dim(key_part, begin_row, sub_rows, 0).reshape(
                sub_rows, kv_local, HD
            )
            values_block = lax.dynamic_slice_in_dim(value_part, begin_row, sub_rows, 0).reshape(
                sub_rows, kv_local, HD
            )
            key_pos = begin_row + jnp.arange(sub_rows, dtype=jnp.int32)
            key_docs = lax.dynamic_slice_in_dim(doc_id, begin_row, sub_rows, 0)
            allowed = (key_pos[None, :] <= query_pos[:, None]) & (
                key_docs[None, :] == query_docs[:, None]
            )
            scores = (
                jnp.einsum(
                    "gjtd,sgd->gjts", queries, keys_block, preferred_element_type=jnp.float32
                )
                * scaling
            )
            new_peak = jnp.maximum(highest, jnp.max(jnp.where(allowed, scores, NEGATIVE), axis=3))
            factor = jnp.exp(highest - new_peak)
            weights = jnp.where(allowed, jnp.exp(scores - new_peak[..., None]), 0.0)
            totals = totals * factor + jnp.sum(weights, axis=3)
            mixture = mixture * factor[..., None] + jnp.einsum(
                "gjts,sgd->gjtd",
                weights.astype(jnp.bfloat16),
                values_block,
                preferred_element_type=jnp.float32,
            )
            return (new_peak, totals, mixture)

        return lax.fori_loop(0, key_count // sub_rows, update_one_block, current)

    def unchanged(current):
        return current

    finished = lax.cond(visible, update, unchanged, start_state)
    outputs = (finished[2] / finished[1][..., None]).astype(jnp.bfloat16)
    return outputs.transpose(2, 0, 1, 3).reshape(tok_rows, kv_local * QPK * HD)


def solution(mesh):
    placed = (
        P("enc", None),
        P("enc"),
        P(),
        P(None, "ctx", None),
        P("ctx", None),
        P(),
        P(None, "ctx"),
        P("ctx", "enc"),
        P("ctx", "enc"),
        P(),
        P(),
        P(),
        P(None, "enc"),
        P(None, "enc"),
        P(None, "enc"),
    )
    return jax.shard_map(
        body, mesh=mesh, in_specs=placed, out_specs=P("ctx", "enc"), check_vma=False
    )
```

profile of v0, /device:TPU:0, one launch (start us, length us, event | category | flops | bytes accessed | tf_op | source)
XLA Modules:
  0.0 467.7 jit_solution(1278942646428029388)
XLA Ops:
  6.6 2.0 convert_reduce_fusion
  11.7 14.6 %while.28 = (s32[]{:T(128)}, bf16[3,2,256,80]{2,3,1,0:T(8,128)(2,1)}, s32[3]{0:T(128)S(1)}, s32[768]{0:T(1024)S(1)}, bf16[2,768,80]{1,2,0:T(8,128)(2,1)S(1)}, /*...) while((s32[]{:T(128)}, ...), condition=%wide.region_5.6_spmd, body=%wide.region_2.5_spmd.sunk | while | flops 128859136 | bytes 6767287 | solution.py:46
  27.2 2.6 fusion.74
  29.9 80.8 %all-reduce.2.cloned.1.call-done = f32[768,1280]{1,0:T(8,128)} async-done(((f32[768,1280]{1,0:T(8,128)}), f32[768,1280]{1,0:T(8,128)}) %all-reduce.2.cloned.1.call-update) | async-done | bytes 3932176 | tf_op jit(solution)/shard_map/psum | solution.py:85
  110.6 3.1 fusion.50
  114.8 2.0 fusion.49
  116.8 4.1 reshape.149
  120.8 6.1 %fusion.61 = bf16[192,640]{1,0:T(8,128)(2,1)S(1)} fusion(bf16[192,5120]{1,0:T(8,128)(2,1)} %reshape.149, bf16[5120,640]{1,0:T(8,128)(2,1)} %param.27), kind=kOutput, calls=%fused_computation.81 | convolution fusion | flops 1266278400 | bytes 8765440 | tf_op jit(solution)/shard_map/dot_general | solution.py:90
  127.0 21.8 %all_gather.15 = bf16[768,640]{1,0:T(8,128)(2,1)S(1)} all-gather(bf16[192,640]{1,0:T(8,128)(2,1)S(1)} %fusion.61), channel_id=1, replica_groups=mesh['enc'=4,'ctx'=8] {'enc'}, dimensions={0}, use_global_device_ids=true | all-gather | bytes 1228800 | tf_op jit(solution)/shard_map/all_gather | solution.py:92
  148.8 4.5 fusion.75
  153.3 60.7 %reduce-scatter.2.cloned.1.call-done = f32[96,2048]{1,0:T(8,128)} async-done(((f32[768,2048]{1,0:T(8,128)}), f32[96,2048]{1,0:T(8,128)}) %reduce-scatter.2.cloned.1.call-update) | async-done | bytes 786448 | tf_op jit(solution)/shard_map/reduce_scatter | solution.py:97
  214.0 1.9 convert_element_type.68
  217.0 31.3 %all-gather.3.cloned.1.call-done = bf16[768,2048]{1,0:T(8,128)(2,1)} async-done(((bf16[96,2048]{1,0:T(8,128)(2,1)}), bf16[768,2048]{1,0:T(8,128)(2,1)}) %all-gather.3.cloned.1.call-update) | async-done | bytes 3145744 | tf_op jit(solution)/shard_map/all_gather | solution.py:103
  248.3 6.7 %gather_fusion = bf16[384,2048]{1,0:T(8,128)(2,1)S(1)} fusion(bf16[768,2048]{1,0:T(8,128)(2,1)} %all-gather.3.cloned.1.call-done, s32[1024]{0:T(1024)S(1)} %pad_clamp_fusion), kind=kCustom, calls=%fused_computation | custom fusion | bytes 3147264 | tf_op jit(solution)/shard_map/jit(_take)/gather | solution.py:104
  260.3 111.6 %all-gather.5.cloned.1.call-done = bf16[384,8192]{1,0:T(8,128)(2,1)} async-done(((bf16[384,2048]{1,0:T(8,128)(2,1)}), bf16[384,8192]{1,0:T(8,128)(2,1)}) %all-gather.5.cloned.1.call-update) | async-done | bytes 6291472 | tf_op jit(solution)/shard_map/all_gather | solution.py:106
  371.9 4.3 fusion.37
  376.5 3.7 convolution_convert_fusion.1
  380.2 11.4 %all_gather.19 = bf16[3072,128]{1,0:T(8,128)(2,1)} all-gather(bf16[384,128]{1,0:T(8,128)(2,1)S(1)} %convolution_convert_fusion.1), channel_id=1, replica_groups=mesh['enc'=4,'ctx'=8] {'ctx'}, dimensions={0}, use_global_device_ids=true | all-gather | bytes 884736 | tf_op jit(solution)/shard_map/all_gather | solution.py:126
  391.6 3.4 convolution_convert_fusion
  396.0 4.6 convolution_convert_fusion.2
  400.6 11.5 %all_gather.18 = bf16[3072,128]{1,0:T(8,128)(2,1)} all-gather(bf16[384,128]{1,0:T(8,128)(2,1)S(1)} %convolution_convert_fusion.2), channel_id=1, replica_groups=mesh['enc'=4,'ctx'=8] {'ctx'}, dimensions={0}, use_global_device_ids=true | all-gather | bytes 884736 | tf_op jit(solution)/shard_map/all_gather | solution.py:125
  412.2 46.3 %conditional.1 = (f32[1,4,384]{2,1,0:T(4,128)}, f32[1,4,384,128]{3,2,1,0:T(8,128)}) conditional(s32[]{:T(128)} %convert_element_type.60, () %tuple.31, (s32[]{:T(128)}, s32[384]{0:T(512)S(1)}, s32[3072]{0:T(1024)}, s32[384]{0:T(512)S(1)}, bf16[3072,128]{1,0:T(8,128)(2,1)}, /*index=5*/bf16[1,4,384,128]{3,2,1,0:T(8,128)(2,1)}, ...), branch_computations={%region_11.12_spmd, %region_12.17_spmd} | conditional | flops 412493696 | bytes 12566875 | solution.py:171
  412.2 46.3 %while.27 = (s32[]{:T(128)}, f32[1,4,384]{2,1,0:T(4,128)S(1)}, f32[1,4,384]{2,1,0:T(4,128)}, f32[1,4,384,128]{3,2,1,0:T(8,128)}, s32[384]{0:T(512)S(1)}, /*index...) while((s32[]{:T(128)}, f32[1,4,384]{2,1,0:T(4,128)S(1)}, ...), condition=%wide.region_16.16_spmd.clone, body=%wide.region_13.15_spmd.clone.sunk | while | flops 412493312 | bytes 12563663 | solution.py:166
  413.2 1.7 fusion.108
  414.9 2.8 fusion.111
  420.1 1.7 fusion.108
  421.8 3.1 fusion.111
  429.7 3.1 fusion.111
  435.8 1.7 fusion.108
  437.6 3.1 fusion.111
  445.5 3.1 fusion.111
  453.4 3.1 fusion.111
  (136 shorter events, 46.1 us)
Async XLA Ops:
  6.5 142.2 %copy-start = (bf16[640,2048]{1,0:T(8,128)(2,1)S(1)}, bf16[640,2048]{1,0:T(8,128)(2,1)}, u32[]{:S(2)}) copy-start(bf16[640,2048]{1,0:T(8,128)(2,1)} %param.28) | copy-start | bytes 7864324
  6.5 3.0 copy-start.12
  6.5 104.1 %all-reduce.2.cloned.1.call-start = ((), (), s32[]{:S(2)}) async-start(), calls=%async_computation.1 | async-start | bytes 7864320 | tf_op jit(solution)/shard_map/psum | solution.py:85
  6.5 2.3 copy-start.2
  6.6 3.0 copy-start.10
  9.5 2.1 copy-start.7
  11.7 15.5 %copy-start.5 = (bf16[160,1280]{1,0:T(8,128)(2,1)S(1)}, bf16[160,1280]{1,0:T(8,128)(2,1)}, u32[]{:S(2)}) copy-start(bf16[160,1280]{1,0:T(8,128)(2,1)} %param.25) | copy-start | bytes 1228804
  13.9 1.4 copy-start.6
  18.8 1.4 copy-start.6
  23.6 1.4 copy-start.6
  29.8 184.1 %reduce-scatter.2.cloned.1.call-start = ((), (), s32[]{:S(2)}) async-start(), calls=%async_computation.2 | async-start | bytes 7077888 | tf_op jit(solution)/shard_map/reduce_scatter | solution.py:97
  113.8 1.0 copy-start.8
  153.2 95.0 %all-gather.3.cloned.1.call-start = ((), (), s32[]{:S(2)}) async-start(), calls=%async_computation.3 | async-start | bytes 3538944 | tf_op jit(solution)/shard_map/all_gather | solution.py:103
  215.9 156.0 %all-gather.5.cloned.1.call-start = ((), (), s32[]{:S(2)}) async-start(), calls=%async_computation.4 | async-start | bytes 7864320 | tf_op jit(solution)/shard_map/all_gather | solution.py:106
  217.0 38.0 %copy-start.4 = (bf16[384,2048]{1,0:T(8,128)(2,1)S(1)}, bf16[384,2048]{1,0:T(8,128)(2,1)}, u32[]{:S(2)}) copy-start(bf16[384,2048]{1,0:T(8,128)(2,1)} %param.29) | copy-start | bytes 4718596
  256.4 119.8 %copy-start.11 = (f32[8192]{0:T(1024)S(1)}, f32[8192]{0:T(1024)}, u32[]{:S(2)}) copy-start(f32[8192]{0:T(1024)} %param.32) | copy-start | bytes 98308
  371.9 4.6 copy-start.3
  371.9 19.7 %slice-start = ((s8[8388608]{0:T(1024)(128)(4,1)}), s8[4194304]{0:T(1024)(128)(4,1)S(1)}, s32[]{:S(2)}) async-start(s8[8388608]{0:T(1024)(128)(4,1)} %bitcast.126), calls=%async_computation.5 | async-start | bytes 8388608
  376.5 15.1 %slice-start.1 = ((s8[8388608]{0:T(1024)(128)(4,1)}), s8[4194304]{0:T(1024)(128)(4,1)S(1)}, s32[]{:S(2)}) async-start(s8[8388608]{0:T(1024)(128)(4,1)} %bitcast.126), calls=%async_computation.6 | async-start | bytes 8388608
  391.6 4.4 copy-start.9
  458.5 2.7 copy-start.1
Sparse Core Ops, SparseCore 0:
  30.0 80.6 all-reduce.1
  153.4 60.5 reduce-scatter.1
  216.0 32.1 all-gather.2
  256.6 115.3 all-gather.4
where the time goes:
time: 469 us; the launch traced here: 468 us
  waiting for transfers between devices  284 us (61%)
  matrix products  60.8 us (13%)
  blocking collectives  44.7 us (10%)
  other arithmetic  33.3 us (7%)
  local copies, waits for them, and re-layouts  24.3 us (5%)
  between operations  14.6 us (3%)
  loops' own time  5.3 us (1%)
    all_gather x1, waiting for transfers between devices, body(): full_rows = lax.all_gather(sequence, 'enc', axis=1, tiled=True)  112 us
    psum x1, waiting for transfers between devices, body(): summed = lax.psum(head_terms, 'ctx')  80.8 us
    reduce_scatter x1, waiting for transfers between devices, body(): lax.psum_scatter(jnp.dot(all_hidden, merge_down, preferred_element_type=j...  60.7 us
    all_gather x1, waiting for transfers between devices, body(): vision_all = lax.all_gather(own_vision, 'ctx', axis=0, tiled=True)  31.3 us
    all_gather x1, blocking collectives, body(): all_hidden = lax.all_gather(hidden, 'enc', axis=0, tiled=True)  21.8 us
    dot_general x6, matrix products, update_one_block(): jnp.einsum('gjts,sgd->gjtd', weights.astype(jnp.bfloat16), values_block,...  18.4 us
    all_gather x1, blocking collectives, body(): key_part = lax.all_gather(keys_local, 'ctx', axis=0, tiled=True)  11.5 us
    all_gather x1, blocking collectives, body(): value_part = lax.all_gather(values_local, 'ctx', axis=0, tiled=True)  11.4 us
  transfers between devices with their start and end apart: 4, of which 4 were waited for; matrix products, arithmetic and copies ran while one was open for 1% of the time, Pallas kernels for 0%

commit v1 on v0

--- a/solution.py
+++ b/solution.py
@@ -103,7 +103,7 @@
     vision_all = lax.all_gather(own_vision, "ctx", axis=0, tiled=True)
     vision_local = jnp.take(vision_all, jnp.clip(local_units, 0, unit_total - 1), axis=0)
     sequence = jnp.where(present[:, None], vision_local, text_embed)
-    full_rows = lax.all_gather(sequence, "enc", axis=1, tiled=True)
+    full_rows = jnp.concatenate(lax.all_gather(sequence, "enc"), axis=1)
     widened = full_rows.astype(jnp.float32)
     row_scale = lax.rsqrt(jnp.mean(widened * widened, axis=1, keepdims=True) + EPSILON)
     normed = (widened * row_scale * dec_gain).astype(jnp.bfloat16)

time: 469 us -> 491 us (1.047)
  other arithmetic: 33.3 us -> 43.1 us
  local copies, waits for them, and re-layouts: 24.3 us -> 33.3 us
    convert_element_type x0 -> x1, other arithmetic: none -> 9.92 us  [body(): normed = (widened * row_scale * dec_gain).astype(jnp.bfloat16)]
    convert_element_type x0 -> x1, local copies, waits for them, and re-layouts: none -> 9.42 us  [body(): widened = full_rows.astype(jnp.float32)]
where the time goes in v1:
time: 491 us; the launch traced here: 490 us
  waiting for transfers between devices  284 us (58%)
  matrix products  64.2 us (13%)
  blocking collectives  44.7 us (9%)
  other arithmetic  43.1 us (9%)
  local copies, waits for them, and re-layouts  33.3 us (7%)
  between operations  14.6 us (3%)
  loops' own time  5.3 us (1%)
    all_gather x1, waiting for transfers between devices, body(): full_rows = jnp.concatenate(lax.all_gather(sequence, 'enc'), axis=1)  112 us
    psum x1, waiting for transfers between devices, body(): summed = lax.psum(head_terms, 'ctx')  80.8 us
    reduce_scatter x1, waiting for transfers between devices, body(): lax.psum_scatter(jnp.dot(all_hidden, merge_down, preferred_element_type=j...  60.7 us
    all_gather x1, waiting for transfers between devices, body(): vision_all = lax.all_gather(own_vision, 'ctx', axis=0, tiled=True)  31.3 us
    all_gather x1, blocking collectives, body(): all_hidden = lax.all_gather(hidden, 'enc', axis=0, tiled=True)  21.8 us
    dot_general x6, matrix products, update_one_block(): jnp.einsum('gjts,sgd->gjtd', weights.astype(jnp.bfloat16), values_block,...  18.4 us
    all_gather x1, blocking collectives, body(): value_part = lax.all_gather(values_local, 'ctx', axis=0, tiled=True)  11.5 us
    all_gather x1, blocking collectives, body(): key_part = lax.all_gather(keys_local, 'ctx', axis=0, tiled=True)  11.4 us
  transfers between devices with their start and end apart: 4, of which 4 were waited for; matrix products, arithmetic and copies ran while one was open for 1% of the time, Pallas kernels for 0%

profile of v1, /device:TPU:0, one launch (start us, length us, event | category | flops | bytes accessed | tf_op | source)
XLA Modules:
  0.0 490.0 jit_solution(17910847157729960992)
XLA Ops:
  6.6 2.0 convert_reduce_fusion
  11.7 14.6 %while.28 = (s32[]{:T(128)}, bf16[3,2,256,80]{2,3,1,0:T(8,128)(2,1)}, s32[3]{0:T(128)S(1)}, s32[768]{0:T(1024)S(1)}, bf16[2,768,80]{1,2,0:T(8,128)(2,1)S(1)}, /*...) while((s32[]{:T(128)}, ...), condition=%wide.region_5.6_spmd, body=%wide.region_2.5_spmd.sunk | while | flops 128859136 | bytes 6767287 | solution.py:46
  27.2 2.6 fusion.70
  29.9 80.8 %all-reduce.2.cloned.1.call-done = f32[768,1280]{1,0:T(8,128)} async-done(((f32[768,1280]{1,0:T(8,128)}), f32[768,1280]{1,0:T(8,128)}) %all-reduce.2.cloned.1.call-update) | async-done | bytes 3932176 | tf_op jit(solution)/shard_map/psum | solution.py:85
  110.6 3.1 fusion.49
  114.8 2.0 fusion.48
  116.8 4.1 reshape.153
  120.8 6.1 %fusion.60 = bf16[192,640]{1,0:T(8,128)(2,1)S(1)} fusion(bf16[192,5120]{1,0:T(8,128)(2,1)} %reshape.153, bf16[5120,640]{1,0:T(8,128)(2,1)} %param.27), kind=kOutput, calls=%fused_computation.80 | convolution fusion | flops 1266278400 | bytes 8765440 | tf_op jit(solution)/shard_map/dot_general | solution.py:90
  127.0 21.8 %all_gather.18 = bf16[768,640]{1,0:T(8,128)(2,1)S(1)} all-gather(bf16[192,640]{1,0:T(8,128)(2,1)S(1)} %fusion.60), channel_id=1, replica_groups=mesh['enc'=4,'ctx'=8] {'enc'}, dimensions={0}, use_global_device_ids=true | all-gather | bytes 1228800 | tf_op jit(solution)/shard_map/all_gather | solution.py:92
  148.8 4.5 fusion.71
  153.3 60.7 %reduce-scatter.2.cloned.1.call-done = f32[96,2048]{1,0:T(8,128)} async-done(((f32[768,2048]{1,0:T(8,128)}), f32[96,2048]{1,0:T(8,128)}) %reduce-scatter.2.cloned.1.call-update) | async-done | bytes 786448 | tf_op jit(solution)/shard_map/reduce_scatter | solution.py:97
  214.0 1.9 convert_element_type.78
  217.0 31.3 %all-gather.4.cloned.1.call-done = bf16[768,2048]{1,0:T(8,128)(2,1)} async-done(((bf16[96,2048]{1,0:T(8,128)(2,1)}), bf16[768,2048]{1,0:T(8,128)(2,1)}) %all-gather.4.cloned.1.call-update) | async-done | bytes 3145744 | tf_op jit(solution)/shard_map/all_gather | solution.py:103
  248.3 6.7 %gather_fusion = bf16[384,2048]{1,0:T(8,128)(2,1)S(1)} fusion(bf16[768,2048]{1,0:T(8,128)(2,1)} %all-gather.4.cloned.1.call-done, s32[1024]{0:T(1024)S(1)} %pad_clamp_fusion), kind=kCustom, calls=%fused_computation | custom fusion | bytes 3147264 | tf_op jit(solution)/shard_map/jit(_take)/gather | solution.py:104
  260.3 111.6 %all-gather.6.cloned.1.call-done = bf16[1536,2048]{1,0:T(8,128)(2,1)} async-done(((bf16[384,2048]{1,0:T(8,128)(2,1)}), bf16[1536,2048]{1,0:T(8,128)(2,1)}) %all-gather.6.cloned.1.call-update) | async-done | bytes 6291472 | tf_op jit(solution)/shard_map/all_gather | solution.py:106
  371.9 9.4 %copy.23 = f32[4,384,2048]{1,2,0:T(8,128)} copy(bf16[4,384,2048]{2,1,0:T(8,128)(2,1)} %bitcast.132) | data formatting | bytes 18874368 | tf_op jit(solution)/shard_map/convert_element_type | solution.py:107
  381.3 4.3 multiply_reduce_fusion
  385.6 9.9 %fusion.38 = bf16[384,8192]{0,1:T(8,128)(2,1)} fusion(f32[4,384,2048]{1,2,0:T(8,128)} %copy.23, f32[8192]{0:T(1024)S(1)} %copy-done.7, f32[384]{0:T(512)S(1)} %add_rsqrt_fusion.2), kind=kLoop, calls=%fused_computation.48 | loop fusion | flops 9437184 | bytes 18908672 | tf_op jit(solution)/shard_map/convert_element_type | solution.py:109
  395.6 5.7 %convolution_convert_fusion = bf16[384,512]{1,0:T(8,128)(2,1)S(1)} fusion(bf16[384,8192]{0,1:T(8,128)(2,1)} %fusion.38, bf16[8192,512]{1,0:T(8,128)(2,1)S(1)} %bitcast.135), kind=kOutput, calls=%fused_computation.72 | convolution fusion | flops 3221422080 | bytes 15073280 | tf_op jit(solution)/shard_map/dot_general | solution.py:110
  402.2 4.8 convolution_convert_fusion.2
  407.0 11.4 %all_gather.22 = bf16[3072,128]{1,0:T(8,128)(2,1)} all-gather(bf16[384,128]{1,0:T(8,128)(2,1)S(1)} %convolution_convert_fusion.2), channel_id=1, replica_groups=mesh['enc'=4,'ctx'=8] {'ctx'}, dimensions={0}, use_global_device_ids=true | all-gather | bytes 884736 | tf_op jit(solution)/shard_map/all_gather | solution.py:125
  418.4 4.7 convolution_convert_fusion.1
  423.1 11.5 %all_gather.23 = bf16[3072,128]{1,0:T(8,128)(2,1)} all-gather(bf16[384,128]{1,0:T(8,128)(2,1)S(1)} %convolution_convert_fusion.1), channel_id=1, replica_groups=mesh['enc'=4,'ctx'=8] {'ctx'}, dimensions={0}, use_global_device_ids=true | all-gather | bytes 884736 | tf_op jit(solution)/shard_map/all_gather | solution.py:126
  434.5 46.2 %conditional.1 = (f32[1,4,384]{2,1,0:T(4,128)}, f32[1,4,384,128]{3,2,1,0:T(8,128)}) conditional(s32[]{:T(128)} %convert_element_type.70, () %tuple.31, (s32[]{:T(128)}, s32[384]{0:T(512)S(1)}, s32[3072]{0:T(1024)}, s32[384]{0:T(512)S(1)}, bf16[3072,128]{1,0:T(8,128)(2,1)}, /*index=5*/bf16[1,4,384,128]{3,2,1,0:T(8,128)(2,1)}, ...), branch_computations={%region_11.12_spmd, %region_12.17_spmd} | conditional | flops 412493696 | bytes 12566875 | solution.py:171
  434.6 46.2 %while.27 = (s32[]{:T(128)}, f32[1,4,384]{2,1,0:T(4,128)S(1)}, f32[1,4,384]{2,1,0:T(4,128)}, f32[1,4,384,128]{3,2,1,0:T(8,128)}, s32[384]{0:T(512)S(1)}, /*index...) while((s32[]{:T(128)}, f32[1,4,384]{2,1,0:T(4,128)S(1)}, ...), condition=%wide.region_16.16_spmd.clone, body=%wide.region_13.15_spmd.clone.sunk | while | flops 412493312 | bytes 12563663 | solution.py:166
  437.3 2.8 fusion.110
  442.4 1.7 fusion.107
  444.2 3.1 fusion.110
  452.1 3.1 fusion.110
  460.0 3.1 fusion.110
  467.8 3.1 fusion.110
  475.7 3.1 fusion.110
  (138 shorter events, 49.1 us)
Async XLA Ops:
  6.5 142.2 %copy-start = (bf16[640,2048]{1,0:T(8,128)(2,1)S(1)}, bf16[640,2048]{1,0:T(8,128)(2,1)}, u32[]{:S(2)}) copy-start(bf16[640,2048]{1,0:T(8,128)(2,1)} %param.28) | copy-start | bytes 7864324
  6.5 3.0 copy-start.12
  6.5 104.1 %all-reduce.2.cloned.1.call-start = ((), (), s32[]{:S(2)}) async-start(), calls=%async_computation.1 | async-start | bytes 7864320 | tf_op jit(solution)/shard_map/psum | solution.py:85
  6.5 2.3 copy-start.2
  6.6 3.0 copy-start.11
  9.5 2.1 copy-start.6
  11.7 15.5 %copy-start.4 = (bf16[160,1280]{1,0:T(8,128)(2,1)S(1)}, bf16[160,1280]{1,0:T(8,128)(2,1)}, u32[]{:S(2)}) copy-start(bf16[160,1280]{1,0:T(8,128)(2,1)} %param.25) | copy-start | bytes 1228804
  13.9 1.4 copy-start.5
  18.8 1.4 copy-start.5
  23.6 1.4 copy-start.5
  29.8 184.1 %reduce-scatter.2.cloned.1.call-start = ((), (), s32[]{:S(2)}) async-start(), calls=%async_computation.2 | async-start | bytes 7077888 | tf_op jit(solution)/shard_map/reduce_scatter | solution.py:97
  113.8 1.0 copy-start.8
  153.2 95.0 %all-gather.4.cloned.1.call-start = ((), (), s32[]{:S(2)}) async-start(), calls=%async_computation.3 | async-start | bytes 3538944 | tf_op jit(solution)/shard_map/all_gather | solution.py:103
  215.9 156.0 %all-gather.6.cloned.1.call-start = ((), (), s32[]{:S(2)}) async-start(), calls=%async_computation.4 | async-start | bytes 7864320 | tf_op jit(solution)/shard_map/all_gather | solution.py:106
  217.0 38.0 %copy-start.3 = (bf16[384,2048]{1,0:T(8,128)(2,1)S(1)}, bf16[384,2048]{1,0:T(8,128)(2,1)}, u32[]{:S(2)}) copy-start(bf16[384,2048]{1,0:T(8,128)(2,1)} %param.29) | copy-start | bytes 4718596
  381.3 4.3 copy-start.7
  381.3 14.2 %slice-start = ((s8[8388608]{0:T(1024)(128)(4,1)}), s8[4194304]{0:T(1024)(128)(4,1)S(1)}, s32[]{:S(2)}) async-start(s8[8388608]{0:T(1024)(128)(4,1)} %bitcast.134), calls=%async_computation.5 | async-start | bytes 8388608
  385.6 9.9 %slice-start.1 = ((s8[8388608]{0:T(1024)(128)(4,1)}), s8[4194304]{0:T(1024)(128)(4,1)S(1)}, s32[]{:S(2)}) async-start(s8[8388608]{0:T(1024)(128)(4,1)} %bitcast.134), calls=%async_computation.6 | async-start | bytes 8388608
  395.6 6.6 %copy-start.9 = (bf16[8192,128]{1,0:T(8,128)(2,1)S(1)}, bf16[8192,128]{1,0:T(8,128)(2,1)}, u32[]{:S(2)}) copy-start(bf16[8192,128]{1,0:T(8,128)(2,1)} %param.34) | copy-start | bytes 6291460
  402.2 16.2 %copy-start.10 = (bf16[8192,128]{1,0:T(8,128)(2,1)S(1)}, bf16[8192,128]{1,0:T(8,128)(2,1)}, u32[]{:S(2)}) copy-start(bf16[8192,128]{1,0:T(8,128)(2,1)} %param.35) | copy-start | bytes 6291460
  480.8 2.7 copy-start.1
Sparse Core Ops, SparseCore 0:
  30.0 80.6 all-reduce.1
  153.4 60.5 reduce-scatter.1
  216.0 32.1 all-gather.3
  256.6 115.3 all-gather.5
